TPU v7x, 32 devices: a whole 2x2x4 slice. The times are simulated.
32 devices in a mesh: dp: 32 (over z, y, x, core).
Axes of the slice: x: 2, y: 2, z: 4, core: 2. Of those that a mesh axis runs over, the one named last changes fastest.
Arguments:
- grads: bfloat16 [64, 1024, 1024], P('dp'), may hold values from -6 to 6
- memory: bfloat16 [64, 1024, 1024], P('dp'), may hold values from -6 to 6
- block_ids: int32 [16], replicated, may hold values from 0 to 63, as said below
- layer_ids: int32 [16], replicated, may hold values from 0 to 1, as said below
- master: float32 [128, 16384], P(None, 'dp'), may hold values from -8 to 8
- first_moment: float32 [128, 16384], P(None, 'dp'), may hold values from -8 to 8
- second_moment: float32 [128, 16384], P(None, 'dp'), may hold values from 0.25 to 4
Outputs:
- new_memory: bfloat16 [64, 1024, 1024], P('dp')
- master_new: float32 [128, 16384], P(None, 'dp')
- first_new: float32 [128, 16384], P(None, 'dp')
- second_new: float32 [128, 16384], P(None, 'dp')
- step_blocks: bfloat16 [16, 16384], replicated
Inputs may be any that keep to these rules, and one draw needn't show every extreme that they name: Block ids number the 64 tiles of a layer, and the pairs (layer_ids[k], block_ids[k]) are distinct. `layer_ids`: every layer is named by at least a quarter of the 16 entries, rounded down.
All inputs are finite; a program needn't handle non-finite values.
Results may differ from a plain program's by a relative error of at most 0.0004.
Values may be sent and summed in bfloat16 or wider, within the bound.
A program may use at most 64 MiB of HBM per device.

v0:
```python
import jax
import jax.numpy as jnp
from jax import lax
from jax.sharding import PartitionSpec as P

TILE = 128
filter_rate = 0.3
beta_one = 0.9
beta_two = 0.999
adam_eps = 1e-06
weight_decay = 0.01
learn_rate = 0.01
norm_eps = 1e-06


def take_tiles(source, layer_ids, tile_row, tile_col):

    def single(layer_id, row_tile, col_tile):
        return lax.dynamic_slice(
            source, (layer_id, row_tile * TILE, col_tile * TILE), (1, TILE, TILE)
        )[0]

    return jax.vmap(single)(layer_ids, tile_row, tile_col)


def pack_blocks(grads_dev, memory_dev, layer_ids, tile_row, tile_col):
    grad_tiles = take_tiles(grads_dev, layer_ids, tile_row, tile_col).astype(jnp.float32)
    memory_tiles = take_tiles(memory_dev, layer_ids, tile_row, tile_col).astype(jnp.float32)
    combined = grad_tiles + memory_tiles
    return combined.reshape(combined.shape[0], TILE * TILE)


def selected_mask(layer_ids, block_ids, layers, tile_count):
    columns = layer_ids * (tile_count * tile_count) + block_ids
    all_columns = jnp.arange(layers * tile_count * tile_count, dtype=jnp.int32)
    chosen = jnp.any(columns[:, None] == all_columns[None, :], axis=0)
    return chosen.reshape(layers, tile_count, 1, tile_count, 1)


def filter_memory(grads_dev, memory_dev, chosen):
    layers, model_width, _ = grads_dev.shape
    tile_count = model_width // TILE
    accumulated = grads_dev.astype(jnp.float32) + memory_dev.astype(jnp.float32)
    shaped = accumulated.reshape(layers, tile_count, TILE, tile_count, TILE)
    filtered = jnp.where(chosen, jnp.float32(0.0), shaped).reshape(layers, model_width, model_width)
    mixed = (1.0 - filter_rate) * memory_dev.astype(jnp.float32) + filter_rate * filtered
    return mixed.astype(jnp.bfloat16)


def adam_rows(summed, weights_sel, first_old, second_old):
    first_sel = beta_one * first_old + (1.0 - beta_one) * summed
    second_sel = beta_two * second_old + (1.0 - beta_two) * summed * summed
    update = first_sel / (jnp.sqrt(second_sel) + adam_eps) + weight_decay * weights_sel
    return (first_sel, second_sel, update)


def layer_squares(member, values):
    return jnp.sum(member * jnp.sum(values * values, axis=1)[:, None], axis=0)


def trust_rows(member, weight_total, update_total):
    trust_ratio = jnp.sqrt(weight_total / (update_total + norm_eps))
    return jnp.sum(member * trust_ratio[None, :], axis=1)


def on_device(grads, memory, block_ids, layer_ids, master, first_moment, second_moment):
    layers, model_width, _ = grads.shape
    tile_count = model_width // TILE
    tile_row = block_ids // tile_count
    tile_col = block_ids % tile_count
    columns = layer_ids * (tile_count * tile_count) + block_ids
    member = (layer_ids[:, None] == jnp.arange(layers, dtype=jnp.int32)[None, :]).astype(
        jnp.float32
    )
    weights_sel = jnp.take(master, columns, axis=0)
    first_old = jnp.take(first_moment, columns, axis=0)
    second_old = jnp.take(second_moment, columns, axis=0)
    packed = pack_blocks(grads, memory, layer_ids, tile_row, tile_col)
    summed = lax.psum_scatter(packed, "dp", scatter_dimension=1, tiled=True)
    first_sel, second_sel, update = adam_rows(summed, weights_sel, first_old, second_old)
    weight_total, update_total = lax.psum(
        (layer_squares(member, weights_sel), layer_squares(member, update)), "dp"
    )
    scaled = trust_rows(member, weight_total, update_total)[:, None] * update
    step_blocks = lax.all_gather(scaled.astype(jnp.bfloat16), "dp", axis=1, tiled=True)
    new_memory = filter_memory(
        grads, memory, selected_mask(layer_ids, block_ids, layers, tile_count)
    )
    master_new = master.at[columns].set(weights_sel - learn_rate * scaled)
    first_new = first_moment.at[columns].set(first_sel)
    second_new = second_moment.at[columns].set(second_sel)
    return (new_memory, master_new, first_new, second_new, step_blocks)


def solution(mesh):
    in_specs = (
        P("dp", None, None),
        P("dp", None, None),
        P(),
        P(),
        P(None, "dp"),
        P(None, "dp"),
        P(None, "dp"),
    )
    out_specs = (P("dp", None, None), P(None, "dp"), P(None, "dp"), P(None, "dp"), P())
    return jax.shard_map(
        on_device, mesh=mesh, in_specs=in_specs, out_specs=out_specs, check_vma=False
    )
```

profile of v0, /device:TPU:0, one launch (start us, length us, event | category | flops | bytes accessed | tf_op | source)
XLA Modules:
  0.0 355.8 jit_solution(294397355076881631)
XLA Ops:
  10.9 56.7 %while.3 = (s32[]{:T(128)}, bf16[2,1024,1024]{2,1,0:T(8,128)(2,1)}, s32[16,3]{0,1:T(4,128)S(1)}, bf16[16,1,128,128]{3,2,1,0:T(8,128)(2,1)S(1)}, s32[]{:T(128)}) while((s32[]{:T(128)}, bf16[2,1024,1024]{2,1,0:T(8,128)(2,1)}, s32[16,3]{0,1:T(4,128)S(1)}, bf16[16,1,128,128]{3,2,1,0:T(8,128)(2,1)S(1)}, s32[]{:T(128)}) %tuple.46), condition=%wide.while_cond.1, body=%wide.while_body.1.sunk | while | flops 2 | bytes 65673 | solution.py:19
  11.5 2.9 bitcast_dynamic-update-slice_fusion.5
  18.6 2.9 bitcast_dynamic-update-slice_fusion.5
  22.2 2.9 bitcast_dynamic-update-slice_fusion.5
  25.7 2.9 bitcast_dynamic-update-slice_fusion.5
  29.2 2.9 bitcast_dynamic-update-slice_fusion.5
  32.8 2.9 bitcast_dynamic-update-slice_fusion.5
  36.3 2.9 bitcast_dynamic-update-slice_fusion.5
  39.9 2.9 bitcast_dynamic-update-slice_fusion.5
  43.4 2.9 bitcast_dynamic-update-slice_fusion.5
  50.5 2.9 bitcast_dynamic-update-slice_fusion.5
  54.1 2.9 bitcast_dynamic-update-slice_fusion.5
  61.1 2.9 bitcast_dynamic-update-slice_fusion.5
  64.7 2.9 bitcast_dynamic-update-slice_fusion.5
  67.7 56.7 %while.2 = (s32[]{:T(128)}, bf16[2,1024,1024]{2,1,0:T(8,128)(2,1)}, s32[16,3]{0,1:T(4,128)S(1)}, bf16[16,1,128,128]{3,2,1,0:T(8,128)(2,1)S(1)}, s32[]{:T(128)}) while((s32[]{:T(128)}, bf16[2,1024,1024]{2,1,0:T(8,128)(2,1)}, s32[16,3]{0,1:T(4,128)S(1)}, bf16[16,1,128,128]{3,2,1,0:T(8,128)(2,1)S(1)}, s32[]{:T(128)}) %tuple.56), condition=%wide.while_cond, body=%wide.while_body.sunk | while | flops 2 | bytes 65673 | solution.py:19
  68.3 2.9 bitcast_dynamic-update-slice_fusion.4
  71.9 2.9 bitcast_dynamic-update-slice_fusion.4
  75.4 2.9 bitcast_dynamic-update-slice_fusion.4
  82.5 2.9 bitcast_dynamic-update-slice_fusion.4
  128.4 5.3 %broadcast_in_dim.52 = pred[2,1024,1024]{2,1,0:T(8,128)(4,1)S(1)} reshape(pred[2,8,128,8,128]{4,3,2,1,0:T(8,128)(4,1)} %broadcast_in_dim.51) | data formatting | bytes 4194304 | tf_op jit(solution)/shard_map/jit(_where)/broadcast_in_dim | solution.py:45
  135.4 6.2 %fusion.1 = bf16[2,1024,1024]{2,1,0:T(8,128)(2,1)} fusion(bf16[2,1024,1024]{2,1,0:T(8,128)(2,1)} %get-tuple-element.159, pred[2,1024,1024]{2,1,0:T(8,128)(4,1)S(1)} %broadcast_in_dim.52, bf16[2,1024,1024]{2,1,0:T(8,128)(2,1)} %get-tuple-element.160), kind=kLoop, calls=%fused_computation.13 | loop fusion | flops 16777216 | bytes 14680064 | tf_op jit(solution)/shard_map/convert_element_type | solution.py:47
  141.6 124.0 %reduce-scatter.2.cloned.1.call-done = f32[16,512]{1,0:T(8,128)} async-done(((f32[16,16384]{1,0:T(8,128)}), f32[16,512]{1,0:T(8,128)}) %reduce-scatter.2.cloned.1.call-update) | async-done | bytes 32784 | tf_op jit(solution)/shard_map/reduce_scatter | solution.py:79
  266.7 36.9 %all-reduce = (f32[2]{0:T(128)S(1)}, f32[2]{0:T(128)S(1)}) all-reduce(f32[2]{0:T(128)S(1)} %get-tuple-element.23, f32[2]{0:T(128)S(1)} %get-tuple-element.22), channel_id=1, replica_groups=mesh['dp'=32] {'dp'}, use_global_device_ids=true, to_apply=%region_3.5 | all-reduce | flops 4 | bytes 32 | tf_op jit(solution)/shard_map/psum | solution.py:81
  303.7 41.3 %all_gather.3 = bf16[16,16384]{1,0:T(8,128)(2,1)S(1)} all-gather(bf16[16,512]{1,0:T(8,128)(2,1)S(1)} %multiply_convert_fusion), channel_id=1, replica_groups=mesh['dp'=32] {'dp'}, dimensions={1}, use_global_device_ids=true | all-gather | bytes 540672 | tf_op jit(solution)/shard_map/all_gather | solution.py:85
  (118 shorter events, 77.7 us)
Async XLA Ops:
  7.2 258.4 %reduce-scatter.2.cloned.1.call-start = ((), (), s32[]{:S(2)}) async-start(), calls=%async_computation.1 | async-start | bytes 1081344 | tf_op jit(solution)/shard_map/reduce_scatter | solution.py:79
  8.2 118.0 %copy-start.3 = (s32[16]{0:T(128)S(1)}, s32[16]{0:T(128)}, u32[]{:S(2)}) copy-start(s32[16]{0:T(128)} %param.12) | copy-start | bytes 196
  8.2 118.0 %copy-start.4 = (s32[16]{0:T(128)S(1)}, s32[16]{0:T(128)}, u32[]{:S(2)}) copy-start(s32[16]{0:T(128)} %param.11) | copy-start | bytes 196
  345.8 3.1 copy-start.2
  347.0 2.0 copy-start.1
  348.1 0.9 copy-start
Sparse Core Ops, SparseCore 0:
  126.3 139.2 reduce-scatter.1
where the time goes:
time: 359 us; the launch traced here: 356 us
  local copies, waits for them, and re-layouts  127 us (35%)
  waiting for transfers between devices  124 us (35%)
  blocking collectives  78.1 us (22%)
  between operations  14.2 us (4%)
  other arithmetic  11.5 us (3%)
    reduce_scatter x1, waiting for transfers between devices, on_device(): summed = lax.psum_scatter(packed, 'dp', scatter_dimension=1, tiled=True)  124 us
    gather x96, local copies, waits for them, and re-layouts  113 us
    all_gather x1, blocking collectives, on_device(): lax.all_gather(scaled.astype(jnp.bfloat16), 'dp', axis=1, tiled=True)  41.3 us
    psum x1, blocking collectives, on_device(): lax.psum((layer_squares(member, weights_sel), layer_squares(member, updat...  36.9 us
    broadcast_in_dim x3, local copies, waits for them, and re-layouts, filter_memory(): jnp.where(chosen, jnp.float32(0.0), shaped)  7.3 us
  transfers between devices with their start and end apart: 1, of which 1 were waited for; matrix products, arithmetic and copies ran while one was open for 4% of the time, Pallas kernels for 0%

commit v1 on v0

--- a/solution.py
+++ b/solution.py
@@ -82,7 +82,12 @@
         (layer_squares(member, weights_sel), layer_squares(member, update)), "dp"
     )
     scaled = trust_rows(member, weight_total, update_total)[:, None] * update
-    step_blocks = lax.all_gather(scaled.astype(jnp.bfloat16), "dp", axis=1, tiled=True)
+    array = scaled.astype(jnp.bfloat16)
+    count = lax.axis_size("dp")
+    repeats = [count if d == 1 else 1 for d in range(array.ndim)]
+    step_blocks = lax.all_to_all(
+        jnp.tile(array, repeats), "dp", split_axis=1, concat_axis=1, tiled=True
+    )
     new_memory = filter_memory(
         grads, memory, selected_mask(layer_ids, block_ids, layers, tile_count)
     )

time: 359 us -> 337 us (0.939)
  blocking collectives: 78.1 us -> 36.9 us
  waiting for transfers between devices: 124 us -> 138 us
  starting transfers between devices: 0.04 us -> 5.06 us
    all_gather x1 -> x0, blocking collectives: 41.3 us -> none  [on_device(): lax.all_gather(scaled.astype(jnp.bfloat16), 'dp', axis=1, tiled=True)]
    reduce_scatter x1, waiting for transfers between devices: 124 us -> 138 us  [on_device(): summed = lax.psum_scatter(packed, 'dp', scatter_dimension=1, tiled=True)]
    all_to_all x0 -> x1, starting transfers between devices: none -> 5.02 us  [on_device(): lax.all_to_all(jnp.tile(array, repeats), 'dp', split_axis=1, concat_axis=...]
  transfers between devices with their start and end apart: 1 -> 2, of which waited for: 1 -> 1; matrix products, arithmetic and copies ran while one was open for 4% -> 5% of each run, Pallas kernels for 0% -> 0%
where the time goes in v1:
time: 337 us; the launch traced here: 334 us
  waiting for transfers between devices  138 us (41%)
  local copies, waits for them, and re-layouts  128 us (38%)
  blocking collectives  36.9 us (11%)
  between operations  14.2 us (4%)
  other arithmetic  11.2 us (3%)
  starting transfers between devices  5.06 us (2%)
    reduce_scatter x1, waiting for transfers between devices, on_device(): summed = lax.psum_scatter(packed, 'dp', scatter_dimension=1, tiled=True)  138 us
    gather x96, local copies, waits for them, and re-layouts  113 us
    psum x1, blocking collectives, on_device(): lax.psum((layer_squares(member, weights_sel), layer_squares(member, updat...  36.9 us
    broadcast_in_dim x3, local copies, waits for them, and re-layouts, filter_memory(): jnp.where(chosen, jnp.float32(0.0), shaped)  7.3 us
  transfers between devices with their start and end apart: 2, of which 1 were waited for; matrix products, arithmetic and copies ran while one was open for 5% of the time, Pallas kernels for 0%

profile of v1, /device:TPU:0, one launch (start us, length us, event | category | flops | bytes accessed | tf_op | source)
XLA Modules:
  0.0 333.8 jit_solution(5854893425249265329)
XLA Ops:
  10.9 56.7 %while.3 = (s32[]{:T(128)}, bf16[2,1024,1024]{2,1,0:T(8,128)(2,1)}, s32[16,3]{0,1:T(4,128)S(1)}, bf16[16,1,128,128]{3,2,1,0:T(8,128)(2,1)S(1)}, s32[]{:T(128)}) while((s32[]{:T(128)}, bf16[2,1024,1024]{2,1,0:T(8,128)(2,1)}, s32[16,3]{0,1:T(4,128)S(1)}, bf16[16,1,128,128]{3,2,1,0:T(8,128)(2,1)S(1)}, s32[]{:T(128)}) %tuple.46), condition=%wide.while_cond.1, body=%wide.while_body.1.sunk | while | flops 2 | bytes 65673 | solution.py:19
  11.5 2.9 bitcast_dynamic-update-slice_fusion.5
  18.6 2.9 bitcast_dynamic-update-slice_fusion.5
  22.2 2.9 bitcast_dynamic-update-slice_fusion.5
  25.7 2.9 bitcast_dynamic-update-slice_fusion.5
  29.2 2.9 bitcast_dynamic-update-slice_fusion.5
  32.8 2.9 bitcast_dynamic-update-slice_fusion.5
  36.3 2.9 bitcast_dynamic-update-slice_fusion.5
  39.9 2.9 bitcast_dynamic-update-slice_fusion.5
  43.4 2.9 bitcast_dynamic-update-slice_fusion.5
  50.5 2.9 bitcast_dynamic-update-slice_fusion.5
  54.1 2.9 bitcast_dynamic-update-slice_fusion.5
  61.1 2.9 bitcast_dynamic-update-slice_fusion.5
  64.7 2.9 bitcast_dynamic-update-slice_fusion.5
  67.7 56.7 %while.2 = (s32[]{:T(128)}, bf16[2,1024,1024]{2,1,0:T(8,128)(2,1)}, s32[16,3]{0,1:T(4,128)S(1)}, bf16[16,1,128,128]{3,2,1,0:T(8,128)(2,1)S(1)}, s32[]{:T(128)}) while((s32[]{:T(128)}, bf16[2,1024,1024]{2,1,0:T(8,128)(2,1)}, s32[16,3]{0,1:T(4,128)S(1)}, bf16[16,1,128,128]{3,2,1,0:T(8,128)(2,1)S(1)}, s32[]{:T(128)}) %tuple.54), condition=%wide.while_cond, body=%wide.while_body.sunk | while | flops 2 | bytes 65673 | solution.py:19
  68.3 2.9 bitcast_dynamic-update-slice_fusion.4
  71.9 2.9 bitcast_dynamic-update-slice_fusion.4
  75.4 2.9 bitcast_dynamic-update-slice_fusion.4
  82.5 2.9 bitcast_dynamic-update-slice_fusion.4
  128.0 137.6 %reduce-scatter.2.cloned.1.call-done = f32[16,512]{1,0:T(8,128)} async-done(((f32[16,16384]{1,0:T(8,128)}), f32[16,512]{1,0:T(8,128)}) %reduce-scatter.2.cloned.1.call-update) | async-done | bytes 32784 | tf_op jit(solution)/shard_map/reduce_scatter | solution.py:79
  266.7 36.9 %all-reduce = (f32[2]{0:T(128)S(1)}, f32[2]{0:T(128)S(1)}) all-reduce(f32[2]{0:T(128)S(1)} %get-tuple-element.23, f32[2]{0:T(128)S(1)} %get-tuple-element.22), channel_id=1, replica_groups=mesh['dp'=32] {'dp'}, use_global_device_ids=true, to_apply=%region_3.5 | all-reduce | flops 4 | bytes 32 | tf_op jit(solution)/shard_map/psum | solution.py:81
  304.6 5.0 %all-to-all-start = ((bf16[16,32,512]{2,0,1:T(8,128)(2,1)}), bf16[16,32,512]{2,0,1:T(8,128)(2,1)S(1)}, u32[]{:S(2)}, u32[]{:S(2)}) async-start(bf16[16,32,512]{2,0,1:T(8,128)(2,1)} %tile.2), calls=%async_computation.1 | async-start | bytes 1048576 | tf_op jit(solution)/shard_map/all_to_all | solution.py:88
  311.7 5.3 %broadcast_in_dim.52 = pred[2,1024,1024]{2,1,0:T(8,128)(4,1)S(1)} reshape(pred[2,8,128,8,128]{4,3,2,1,0:T(8,128)(4,1)} %broadcast_in_dim.51) | data formatting | bytes 4194304 | tf_op jit(solution)/shard_map/jit(_where)/broadcast_in_dim | solution.py:45
  317.0 6.2 %fusion.1 = bf16[2,1024,1024]{2,1,0:T(8,128)(2,1)} fusion(bf16[2,1024,1024]{2,1,0:T(8,128)(2,1)} %get-tuple-element.149, pred[2,1024,1024]{2,1,0:T(8,128)(4,1)S(1)} %broadcast_in_dim.52, bf16[2,1024,1024]{2,1,0:T(8,128)(2,1)} %get-tuple-element.150), kind=kLoop, calls=%fused_computation.13 | loop fusion | flops 16777216 | bytes 14680064 | tf_op jit(solution)/shard_map/convert_element_type | solution.py:47
  (124 shorter events, 78.3 us)
Async XLA Ops:
  7.2 258.4 %reduce-scatter.2.cloned.1.call-start = ((), (), s32[]{:S(2)}) async-start(), calls=%async_computation.2 | async-start | bytes 1081344 | tf_op jit(solution)/shard_map/reduce_scatter | solution.py:79
  8.2 118.0 %copy-start.5 = (s32[16]{0:T(128)S(1)}, s32[16]{0:T(128)}, u32[]{:S(2)}) copy-start(s32[16]{0:T(128)} %param.12) | copy-start | bytes 196
  8.2 118.0 %copy-start.6 = (s32[16]{0:T(128)S(1)}, s32[16]{0:T(128)}, u32[]{:S(2)}) copy-start(s32[16]{0:T(128)} %param.11) | copy-start | bytes 196
  266.5 45.2 %copy-start.4 = (f32[16,512]{1,0:T(8,128)}, f32[16,512]{1,0:T(8,128)S(1)}, u32[]{:S(2)}) copy-start(f32[16,512]{1,0:T(8,128)S(1)} %get-tuple-element.43) | copy-start | bytes 98308
  304.6 21.5 %all-to-all-start = ((bf16[16,32,512]{2,0,1:T(8,128)(2,1)}), bf16[16,32,512]{2,0,1:T(8,128)(2,1)S(1)}, u32[]{:S(2)}, u32[]{:S(2)}) async-start(bf16[16,32,512]{2,0,1:T(8,128)(2,1)} %tile.2), calls=%async_computation.1 | async-start | bytes 1048576 | tf_op jit(solution)/shard_map/all_to_all | solution.py:88
  317.0 7.3 %copy-start.3 = (f32[16,512]{1,0:T(8,128)S(1)}, f32[16,512]{1,0:T(8,128)}, u32[]{:S(2)}) copy-start(f32[16,512]{1,0:T(8,128)} %reduce-scatter.2.cloned.1.call-done) | copy-start | bytes 98308
  324.3 2.6 copy-start.2
  325.2 1.8 copy-start.1
  326.1 0.9 copy-start
Sparse Core Ops, SparseCore 0:
  126.3 139.2 reduce-scatter.1
